TPU v7x, 1024 devices: a whole 4x8x16 slice. The times are simulated.
1024 devices in a mesh: expert: 64 (over x_lo, z, core), blk: 16 (over y, x_hi).
Axes of the slice: x: 4 (x_hi: 2, x_lo: 2; x = x_hi * 2 + x_lo), y: 8, z: 16, core: 2. Of those that a mesh axis runs over, the one named last changes fastest.
Arguments:
- tokens: bfloat16 [32768, 3584], P('expert', 'blk'), may hold values from -6 to 6
- route: int32 [32768, 1], P('expert'), may hold values from 0 to 63; in each aligned block of 512 rows (0 to 511, 512 to 1023, ...) at most 12 rows name the same one
- gate_score: float32 [32768, 1], P('expert'), may hold values from 0.1 to 1
- w_gate: bfloat16 [64, 3584, 2048], P('expert', None, 'blk'), may hold values from -0.09375 to 0.09375
- w_up: bfloat16 [64, 3584, 2048], P('expert', None, 'blk'), may hold values from -0.09375 to 0.09375
- w_down: bfloat16 [64, 2048, 3584], P('expert', 'blk'), may hold values from -0.125 to 0.125
Outputs:
- mixed: bfloat16 [32768, 3584], P('expert', 'blk')
Inputs may be any that keep to these rules, and one draw needn't show every extreme that they name: `route`: among the 512 tokens of one index of expert (aligned blocks of rows), no expert is named more than 12 times, a bound that some block reaches.
All inputs are finite; a program needn't handle non-finite values.
Results may differ from a plain program's by a relative error of at most 0.015.
Values may be sent and summed in bfloat16 or wider, within the bound.
A program may use at most 64 MiB of HBM per device.

v0:
```python
import jax
import jax.numpy as jnp
from jax import lax
from jax.sharding import Mesh
from jax.sharding import PartitionSpec as P

EXPERT = ("expert_0", "expert_1", "expert_2")
BLK = ("blk_0", "blk_1")


def cut_along(value, dim, size):
    before, after = (value.shape[:dim], value.shape[dim + 1 :])
    return jnp.moveaxis(value.reshape(*before, size, -1, *after), dim, 0)


def joined_along(pieces, dim):
    pieces = jnp.moveaxis(pieces, 0, dim)
    shape = pieces.shape
    return pieces.reshape(*shape[:dim], shape[dim] * shape[dim + 1], *shape[dim + 2 :])


def exchange_in_order(pieces, axes, order):
    inside = pieces.shape[1:]
    result = pieces.reshape(*(lax.axis_size(a) for a in axes), *inside)
    for k in order:
        result = lax.all_to_all(result, axes[k], k, k, tiled=True)
    return result.reshape(-1, *inside)


def two_step_exchange(value, groups, order, split_dim, concat_dim):
    size = lax.axis_size(groups[0]) * lax.axis_size(groups[1])
    pieces = cut_along(value, split_dim, size)
    return joined_along(exchange_in_order(pieces, groups, order), concat_dim)


def whole_of(value, axes, dim):
    if not axes:
        return value
    nearer = lax.all_gather(value, axes[-1], axis=dim, tiled=True)
    return whole_of(nearer, axes[:-1], dim)


def summed_rows(value, axes, dim):
    if not axes:
        return value
    nearer = lax.psum_scatter(value, axes[0], scatter_dimension=dim, tiled=True)
    return summed_rows(nearer, axes[1:], dim)


def slot_table(route, groups, capacity):
    count = route.shape[0]
    target = route[:, 0]
    later = lax.broadcasted_iota(jnp.int32, (count, count), 0)
    before = lax.broadcasted_iota(jnp.int32, (count, count), 1) < later
    same = target[:, None] == target[None, :]
    rank = jnp.sum(jnp.where(same & before, 1, 0), axis=1).astype(jnp.int32)
    slot_ids = target * capacity + rank
    positions = lax.broadcasted_iota(jnp.int32, (groups * capacity, count), 0)
    return (positions == slot_ids[None, :]).astype(jnp.bfloat16)


def per_device(tokens, route, gate_score, w_gate, w_up, w_down):
    groups = lax.axis_size(EXPERT)
    count = tokens.shape[0]
    capacity = 3 * count // (2 * groups)
    selector = slot_table(route, groups, capacity)
    outgoing = jnp.dot(selector, tokens, preferred_element_type=jnp.float32).astype(jnp.bfloat16)
    arrived = two_step_exchange(outgoing, (("expert_0", "expert_1"), "expert_2"), (1, 0), 0, 0)
    gate_rows = w_gate[0]
    up_rows = w_up[0]
    down_rows = w_down[0]
    whole = whole_of(arrived, BLK, 1)
    gate_acc = jnp.dot(whole, gate_rows, preferred_element_type=jnp.float32)
    up_acc = jnp.dot(whole, up_rows, preferred_element_type=jnp.float32)
    hidden = (jax.nn.silu(gate_acc) * up_acc).astype(jnp.bfloat16)
    partial_sum = jnp.dot(hidden, down_rows, preferred_element_type=jnp.float32)
    shares = summed_rows(partial_sum.astype(jnp.bfloat16), BLK, 1).astype(jnp.float32)
    back = two_step_exchange(
        shares.astype(jnp.bfloat16), (("expert_0", "expert_1"), "expert_2"), (1, 0), 0, 0
    )
    picked = lax.dot_general(
        selector, back, (((0,), (0,)), ((), ())), preferred_element_type=jnp.float32
    )
    return (picked * gate_score).astype(jnp.bfloat16)


def solution(mesh):
    split = Mesh(
        mesh.devices.reshape(2, 16, 2, 8, 2), ("expert_0", "expert_1", "expert_2", "blk_0", "blk_1")
    )
    return jax.shard_map(
        per_device,
        mesh=split,
        in_specs=(
            P(EXPERT, BLK),
            P(EXPERT, None),
            P(EXPERT, None),
            P(EXPERT, None, BLK),
            P(EXPERT, None, BLK),
            P(EXPERT, BLK, None),
        ),
        out_specs=P(EXPERT, BLK),
        check_vma=False,
    )
```

profile of v0, /device:TPU:1, one launch (start us, length us, event | category | flops | bytes accessed | tf_op | source)
XLA Modules:
  0.0 318.7 jit_solution(1787832286016361166)
XLA Ops:
  6.5 0.0 copy-start
  6.5 0.0 all-gather.2.cloned.1.call-start
  6.5 1.0 select_reduce_fusion
  7.6 0.7 multiply_add_fusion
  8.3 1.4 fusion.2
  9.7 0.2 copy.18
  9.9 0.1 reshape_reshape.12
  10.0 0.2 copy.19
  10.2 17.8 %all_to_all.20 = bf16[32,2,12,224]{3,0,2,1:T(8,128)(2,1)S(1)} all-to-all(bf16[32,2,12,224]{3,0,2,1:T(8,128)(2,1)S(1)} %copy.19), channel_id=1, replica_groups=mesh['expert_0'=2,'expert_1'=16,'expert_2'=2,'blk_0'=8,'blk_1'=2] {'expe..., dimensions={1} | all-to-all | bytes 688128 | tf_op jit(solution)/shard_map/all_to_all | solution.py:26
  28.0 0.4 copy.20
  28.4 32.7 %all_to_all.21 = bf16[32,2,12,224]{3,1,2,0:T(2,128)(2,1)S(1)} all-to-all(bf16[32,2,12,224]{3,1,2,0:T(2,128)(2,1)S(1)} %copy.20), channel_id=1, replica_groups=mesh['expert_0'=2,'expert_1'=16,'expert_2'=2,'blk_0'=8,'blk_1'=2] {'expe..., dimensions={0} | all-to-all | bytes 688128 | tf_op jit(solution)/shard_map/all_to_all | solution.py:26
  61.1 0.0 copy-start.1
  61.1 0.1 copy.21
  61.2 0.2 reshape_reshape.13
  61.4 0.2 copy.22
  61.6 10.6 %all_gather.6 = bf16[768,448]{0,1:T(8,128)(2,1)} all-gather(bf16[768,224]{0,1:T(8,128)(2,1)S(1)} %copy.22), channel_id=1, replica_groups=mesh['expert_0'=2,'expert_1'=16,'expert_2'=2,'blk_0'=8,'blk_1'=2] {'blk_1'}, dimensions={1}, use_global_device_ids=true | all-gather | bytes 1032192 | tf_op jit(solution)/shard_map/all_gather | solution.py:39
  72.2 0.0 all-gather.2.cloned.1.call-update
  72.3 0.0 reduce-scatter.3.cloned.1.call-start
  72.3 69.6 %all-gather.2.cloned.1.call-done = bf16[768,3584]{0,1:T(8,128)(2,1)} async-done(((bf16[768,448]{0,1:T(8,128)(2,1)}), bf16[768,3584]{0,1:T(8,128)(2,1)}) %all-gather.2.cloned.1.call-update) | async-done | bytes 5505040 | tf_op jit(solution)/shard_map/all_gather | solution.py:39
  141.9 4.4 %fusion.10 = f32[768,128]{1,0:T(8,128)S(1)} fusion(bf16[768,3584]{0,1:T(8,128)(2,1)} %all-gather.2.cloned.1.call-done, bf16[1,3584,128]{2,1,0:T(8,128)(2,1)} %param.9), kind=kOutput, calls=%fused_computation.14 | convolution fusion | flops 704643072 | bytes 6815744 | tf_op jit(solution)/shard_map/dot_general | solution.py:73
  146.3 0.0 copy-done
  146.3 0.0 copy-done.1
  146.3 10.8 %convolution_convert_fusion = bf16[768,3584]{0,1:T(8,128)(2,1)} fusion(bf16[768,3584]{0,1:T(8,128)(2,1)} %all-gather.2.cloned.1.call-done, bf16[1,128,3584]{2,1,0:T(8,128)(2,1)S(1)} %copy-done, bf16[1,3584,128]{2,1,0:T(8,128)(2,1)S(1)} %copy-done.1, f32[768,128]{1,0:T(8,128)S(1)} %fusion.10), kind=kOutput, calls=%fused_computation | convolution fusion | flops 1412628480 | bytes 13238272 | tf_op jit(solution)/shard_map/dot_general | solution.py:76
  157.2 0.0 copy-start.2
  157.2 0.0 reduce-scatter.3.cloned.1.call-update
  157.2 0.0 reduce-scatter.5.cloned.1.call-start
  157.2 74.8 %reduce-scatter.3.cloned.1.call-done = bf16[768,448]{0,1:T(8,128)(2,1)} async-done(((bf16[768,3584]{0,1:T(8,128)(2,1)}), bf16[768,448]{0,1:T(8,128)(2,1)}) %reduce-scatter.3.cloned.1.call-update) | async-done | bytes 688144 | tf_op jit(solution)/shard_map/reduce_scatter | solution.py:46
  232.0 0.0 reduce-scatter.5.cloned.1.call-update
  232.1 33.7 %reduce-scatter.5.cloned.1.call-done = bf16[768,224]{0,1:T(8,128)(2,1)} async-done(((bf16[768,448]{0,1:T(8,128)(2,1)}), bf16[768,224]{0,1:T(8,128)(2,1)}) %reduce-scatter.5.cloned.1.call-update) | async-done | bytes 344080 | tf_op jit(solution)/shard_map/reduce_scatter | solution.py:46
  265.8 1.1 copy.23
  266.9 0.1 reshape_reshape.14
  267.0 0.2 copy.24
  267.3 4.5 %all_to_all.22 = bf16[32,2,12,224]{3,0,2,1:T(8,128)(2,1)S(1)} all-to-all(bf16[32,2,12,224]{3,0,2,1:T(8,128)(2,1)S(1)} %copy.24), channel_id=1, replica_groups=mesh['expert_0'=2,'expert_1'=16,'expert_2'=2,'blk_0'=8,'blk_1'=2] {'expe..., dimensions={1} | all-to-all | bytes 688128 | tf_op jit(solution)/shard_map/all_to_all | solution.py:26
  271.8 0.4 copy.25
  272.2 38.5 %all_to_all.23 = bf16[32,2,12,224]{3,1,2,0:T(2,128)(2,1)S(1)} all-to-all(bf16[32,2,12,224]{3,1,2,0:T(2,128)(2,1)S(1)} %copy.25), channel_id=1, replica_groups=mesh['expert_0'=2,'expert_1'=16,'expert_2'=2,'blk_0'=8,'blk_1'=2] {'expe..., dimensions={0} | all-to-all | bytes 688128 | tf_op jit(solution)/shard_map/all_to_all | solution.py:26
  310.7 0.1 copy.26
  310.8 0.2 reshape_reshape.15
  311.0 0.0 copy-done.2
  311.0 1.2 fusion.4
Async XLA Ops:
  6.5 139.8 %copy-start = (bf16[1,128,3584]{2,1,0:T(8,128)(2,1)S(1)}, bf16[1,128,3584]{2,1,0:T(8,128)(2,1)}, u32[]{:S(2)}) copy-start(bf16[1,128,3584]{2,1,0:T(8,128)(2,1)} %param.11) | copy-start | bytes 2752516
  6.5 135.3 %all-gather.2.cloned.1.call-start = ((), (), s32[]{:S(2)}) async-start(), calls=%async_computation.6 | async-start | bytes 6193152 | tf_op jit(solution)/shard_map/all_gather | solution.py:39
  61.1 85.2 %copy-start.1 = (bf16[1,3584,128]{2,1,0:T(8,128)(2,1)S(1)}, bf16[1,3584,128]{2,1,0:T(8,128)(2,1)}, u32[]{:S(2)}) copy-start(bf16[1,3584,128]{2,1,0:T(8,128)(2,1)} %param.10) | copy-start | bytes 2752516
  72.3 159.8 %reduce-scatter.3.cloned.1.call-start = ((), (), s32[]{:S(2)}) async-start(), calls=%async_computation.7 | async-start | bytes 6193152 | tf_op jit(solution)/shard_map/reduce_scatter | solution.py:46
  157.2 153.9 %copy-start.2 = (f32[512,1]{0,1:T(1,128)S(1)}, f32[512,1]{0,1:T(1,128)}, u32[]{:S(2)}) copy-start(f32[512,1]{0,1:T(1,128)} %param.8) | copy-start | bytes 6148
  157.2 108.6 %reduce-scatter.5.cloned.1.call-start = ((), (), s32[]{:S(2)}) async-start(), calls=%async_computation.8 | async-start | bytes 1032192 | tf_op jit(solution)/shard_map/reduce_scatter | solution.py:46
Sparse Core Ops, SparseCore 0:
  72.4 69.4 all-gather.1
  157.3 74.6 reduce-scatter.2
  235.4 30.2 reduce-scatter.4
where the time goes:
time: 319 us
  waiting for transfers between devices  178 us (56%)
  blocking collectives  104 us (33%)
  matrix products  17.9 us (6%)
  between operations  13.2 us (4%)
  local copies, waits for them, and re-layouts  3.54 us (1%)
    reduce_scatter x2, waiting for transfers between devices, summed_rows(): nearer = lax.psum_scatter(value, axes[0], scatter_dimension=dim, tiled=True)  108 us
    all_to_all x4, blocking collectives, exchange_in_order(): result = lax.all_to_all(result, axes[k], k, k, tiled=True)  93.5 us
    all_gather x1, waiting for transfers between devices, whole_of(): nearer = lax.all_gather(value, axes[-1], axis=dim, tiled=True)  69.6 us
    dot_general x1, matrix products, per_device(): partial_sum = jnp.dot(hidden, down_rows, preferred_element_type=jnp.float32)  10.8 us
    all_gather x1, blocking collectives, whole_of(): nearer = lax.all_gather(value, axes[-1], axis=dim, tiled=True)  10.6 us
  transfers between devices with their start and end apart: 3, of which 3 were waited for; matrix products, arithmetic and copies ran while one was open for 0% of the time, Pallas kernels for 0%

commit v1 on v0

v1 whole, which is shorter than its diff:
```python
import functools

import jax
import jax.numpy as jnp
from jax import lax
from jax.experimental import pallas as pl
from jax.experimental.pallas import tpu as pltpu
from jax.sharding import Mesh
from jax.sharding import PartitionSpec as P

EXPERT = ("xl", "z", "core")
BLK = ("y", "xh")
MESH = pl.DeviceIdType.MESH
NZ, NY = 16, 8
EXPERTS, CAP = 64, 12
SLOTS = EXPERTS * CAP
HALF = SLOTS // 2
WIDE = 512
PIECES = 4


def remote(src, dst, send, recv, device):
    return pltpu.make_async_remote_copy(
        src_ref=src, dst_ref=dst, send_sem=send, recv_sem=recv, device_id=device, device_id_type=MESH
    )


def padded_halves(rows, groups):
    width = rows.shape[1]
    low = rows[:, :128]
    high = jnp.concatenate([rows[:, 128:], jnp.zeros((rows.shape[0], 256 - width), rows.dtype)], axis=1)
    return [part.reshape(groups, CAP // 4, 4, 128) for part in (low, high)]


def kernel(
    tok_ref, route_ref, score_ref, wg_ref, wu_ref, wd_ref, out_ref,
    sel, outgoing, arrived, rows, wg2, wu2, relay_g, relay_u, wd2, relay_d, acc, hidden, total,
    leaving, back,
    a_send, a_recv, r_send, r_recv, w_send, w_recv, d_send, d_recv, x_send, x_recv,
    ring_send, ring_recv, hid_send, hid_recv,
):
    xl, z, c = lax.axis_index("xl"), lax.axis_index("z"), lax.axis_index("core")
    y, xh = lax.axis_index("y"), lax.axis_index("xh")
    width = tok_ref.shape[0]
    right = (1 - xl, z, c, y, lax.rem(xh + xl, 2))
    left = (1 - xl, z, c, y, lax.rem(xh + 1 - xl, 2))
    up, down = lax.rem(y + 1, NY), lax.rem(y + NY - 1, NY)
    above, below = (xl, z, c, up, xh), (xl, z, c, down, xh)
    mixed = lax.rem(c + xh, 2)
    started = []

    def start(copy):
        copy.start()
        started.append(copy)

    barrier = pltpu.get_barrier_semaphore()

    def greet(device):
        pl.semaphore_signal(barrier, inc=1, device_id=device, device_id_type=MESH)

    def greet_plane(k, carry):
        zz = lax.rem(z + k, NZ)
        for a in range(2):
            for b in range(2):
                device = (lax.rem(xl + a, 2), zz, lax.rem(c + b, 2), y, c)
                if a == 0 and b == 0:
                    pl.when(k + mixed > 0)(functools.partial(greet, device))
                else:
                    greet(device)
            greet((lax.rem(xl + a, 2), zz, xh, y, 1 - c))
        return carry

    lax.fori_loop(0, NZ, greet_plane, 0)
    for k in range(1, NY):
        greet((xl, z, c, lax.rem(y + k, NY), xh))
    greet(right)
    greet(left)

    count = tok_ref.shape[1]
    target = route_ref[...]
    named = lax.broadcasted_iota(jnp.int32, (EXPERTS, count), 0) == target
    earlier = lax.broadcasted_iota(jnp.int32, (count, count), 0) < lax.broadcasted_iota(
        jnp.int32, (count, count), 1
    )
    before = jnp.dot(
        jnp.where(named, 1.0, 0.0).astype(jnp.bfloat16),
        jnp.where(earlier, 1.0, 0.0).astype(jnp.bfloat16),
        preferred_element_type=jnp.float32,
    )
    rank = jnp.sum(jnp.where(named, before, 0.0), axis=0, keepdims=True)
    slot = target.astype(jnp.float32) * CAP + rank
    place = lax.broadcasted_iota(jnp.int32, (SLOTS, count), 0).astype(jnp.float32)
    sel[...] = jnp.where(place == slot, 1.0, 0.0).astype(jnp.bfloat16)
    slotted = lax.dot_general(
        sel[...], tok_ref[...], (((1,), (1,)), ((), ())), preferred_element_type=jnp.float32
    ).astype(jnp.bfloat16)
    for h, part in enumerate(padded_halves(slotted, EXPERTS)):
        outgoing[h] = part

    pl.semaphore_wait(barrier, 2 * EXPERTS - EXPERTS // 2 + NY + mixed)

    mine = xl * NZ + z

    def far_first(k):
        return lax.rem(z + NZ // 2 + (1 - 2 * lax.rem(k, 2)) * ((k + 1) // 2) + NZ, NZ)

    def dispatch(k, carry):
        zz = far_first(k)
        for a in range(2):
            for b in range(2):
                xx, cc = lax.rem(xl + a, 2), lax.rem(c + b, 2)
                src = outgoing.at[:, (xx * NZ + zz) * 2 + cc]
                dst = arrived.at[xh, :, mine]
                away = remote(src, dst, a_send, a_recv, (xx, zz, cc, y, c))
                if a == 0 and b == 0:
                    pl.when((NZ - 1 - k) + mixed > 0)(away.start)

                    @pl.when((NZ - 1 - k) + mixed == 0)
                    def _():
                        pltpu.make_async_copy(src, dst, a_recv).start()
                else:
                    away.start()
        return carry

    lax.fori_loop(0, NZ, dispatch, 0)

    own_rows = pl.ds(pl.multiple_of(128 * xh, 128), 128)
    other_rows = pl.ds(pl.multiple_of(128 * (1 - xh), 128), 128)

    def columns_of(yy):
        return pl.ds(pl.multiple_of(128 * (7 * (yy // 2) + 3 * lax.rem(yy, 2)), 128), WIDE)

    kept = pltpu.make_async_copy(wd_ref.at[:, columns_of(y)], wd2.at[y, own_rows], d_recv.at[0])
    kept.start()
    spread = []
    for k in (4, 3, 5, 2, 6, 1, 7):
        yy = lax.rem(y + k, NY)
        copy = remote(
            wd_ref.at[:, columns_of(yy)], wd2.at[y, own_rows], d_send.at[k], d_recv.at[k], (xl, z, c, yy, xh)
        )
        start(copy)
        spread.append(k)

    part_rows = wg_ref.shape[0] // PIECES

    def weight_copies(p, hop):
        piece = pl.ds(part_rows * p, part_rows)
        g_src, u_src = (wg_ref, wu_ref) if hop == 0 else (relay_g, relay_u)
        g_dst, u_dst = (relay_g, relay_u) if hop == 0 else (wg2, wu2)
        return (
            remote(g_src.at[piece], g_dst.at[piece], w_send.at[hop, 0, p], w_recv.at[hop, 0, p], right),
            remote(u_src.at[piece], u_dst.at[piece], w_send.at[hop, 1, p], w_recv.at[hop, 1, p], left),
        )

    for p in range(PIECES):
        for copy in weight_copies(p, 0):
            start(copy)

    def relay_weights(p):
        for first, second in zip(weight_copies(p, 0), weight_copies(p, 1)):
            first.wait_recv()
            start(second)

    relay_weights(0)
    pltpu.make_async_copy(arrived, arrived, a_recv).wait()
    for s in range(2):
        for h in range(2):
            rows[y, s, h] = arrived[s, h].reshape(HALF, 128)

    def ring(view, subs, send, recv, work):
        def hop(origin, s, d, j):
            there = above if d == 0 else below
            return remote(view(origin, j), view(origin, j), send.at[d, s, j], recv.at[d, s, j], there)

        for j in range(subs):
            for d in range(2):
                start(hop(y, 0, d, j))
        work(0, y, None)
        for s in range(1, NY // 2 + 1):
            origins = (lax.rem(y - s + NY, NY), lax.rem(y + s, NY))
            for j in range(subs):
                for d in range(2):
                    whole_way = (j < subs // 2) == (d == 0)
                    if s == NY // 2 and not whole_way:
                        continue
                    hop(origins[d], s - 1, d, j).wait_recv()
                    if s < NY // 2 - 1 or (s == NY // 2 - 1 and whole_way):
                        start(hop(origins[d], s, d, j))
            if s < NY // 2:
                work(s, *origins)
            else:
                work(s, origins[0], None)

    def gate_up(origin, which, g_ref, u_ref):
        result = acc[which]
        for s in range(2):
            first_row = pl.ds(pl.multiple_of((2 * origin + s) * width, 32), width)
            values = jnp.concatenate([rows[origin, s, 0], rows[origin, s, 1]], axis=1)[:, :width]
            weights = jnp.concatenate([g_ref[first_row, :], u_ref[first_row, :]], axis=1)
            result = result + jnp.dot(values, weights, preferred_element_type=jnp.float32)
        acc[which] = result

    def first_work(s, one, two):
        if s == 0:
            acc[...] = jnp.zeros_like(acc)
        for origin in (one,) if two is None else (one, two):
            gate_up(origin, 0, wg_ref, wu_ref)
        if 1 <= s < PIECES:
            relay_weights(s)
        if s == 0:
            for k in range(NY):
                wait_spread(k)
        if s == 3:
            for p in range(NY):
                start(down_hop(p, 0))

    def wait_spread(k):
        source = lax.rem(y - k + NY, NY)
        dst = wd2.at[source, own_rows]
        pltpu.make_async_copy(dst, dst, d_recv.at[k]).wait()

    def down_hop(p, hop):
        there = right if p % 2 == 0 else left
        origin_xh = lax.rem(xh + 1 - xl, 2) if p % 2 == 0 else lax.rem(xh + xl, 2)
        if hop == 0:
            return remote(wd2.at[p, own_rows], relay_d.at[p], x_send.at[0, p], x_recv.at[0, p], there)
        there_rows = pl.ds(pl.multiple_of(128 * origin_xh, 128), 128)
        return remote(relay_d.at[p], wd2.at[p, there_rows], x_send.at[1, p], x_recv.at[1, p], there)

    ring(
        lambda origin, j: rows.at[origin, j // 2, j % 2], 4, ring_send, ring_recv, first_work
    )

    for p in range(PIECES):
        for copy in weight_copies(p, 1):
            copy.wait_recv()

    def other_units(k, carry):
        gate_up(k, 1, wg2, wu2)
        return carry

    lax.fori_loop(0, NY, other_units, 0)
    for which, plane in ((0, xh), (1, 1 - xh)):
        gate, value = acc[which, :, :128], acc[which, :, 128:]
        hidden[y, plane] = (gate / (1.0 + jnp.exp(-gate)) * value).astype(jnp.bfloat16)

    def down_relay(p):
        down_hop(p, 0).wait_recv()
        start(down_hop(p, 1))

    def project(origin):
        values = jnp.concatenate([hidden[origin, 0], hidden[origin, 1]], axis=1)
        total[...] += jnp.dot(values, wd2[origin], preferred_element_type=jnp.float32)

    def second_work(s, one, two):
        if s < 4:
            down_relay(2 * s)
            down_relay(2 * s + 1)

    ring(
        lambda origin, j: hidden.at[origin, j // 2, pl.ds(HALF // 2 * (j % 2), HALF // 2)],
        4, hid_send, hid_recv, second_work,
    )
    for p in range(NY):
        dst = wd2.at[p, other_rows]
        pltpu.make_async_copy(dst, dst, x_recv.at[1, p]).wait()
    total[...] = jnp.zeros_like(total)

    def projections(k, carry):
        project(k)
        return carry

    lax.fori_loop(0, NY, projections, 0)
    summed = total[...]
    summed = jnp.where(lax.rem(y, 2) == 1, summed[:, WIDE - 2 * width :], summed[:, : 2 * width])
    for s in range(2):
        share = summed[:, s * width : (s + 1) * width].astype(jnp.bfloat16)
        for h, part in enumerate(padded_halves(share, EXPERTS // 2)):
            leaving[s, h] = part

    expert = mine * 2 + c

    def give_back(k, carry):
        zz = far_first(k)
        for a in range(2):
            for b in range(2):
                xx, there = lax.rem(xl + a, 2), lax.rem(xh + b, 2)
                src = leaving.at[there, :, xx * NZ + zz]
                dst = back.at[:, expert]
                away = remote(src, dst, r_send, r_recv, (xx, zz, xh, y, there))
                if a == 0 and b == 0:
                    pl.when((NZ - 1 - k) + mixed > 0)(away.start)

                    @pl.when((NZ - 1 - k) + mixed == 0)
                    def _():
                        pltpu.make_async_copy(src, dst, r_recv).start()
                else:
                    away.start()
        return carry

    lax.fori_loop(0, NZ, give_back, 0)
    pltpu.make_async_copy(back, back, r_recv).wait()
    returned = jnp.concatenate([back[h].reshape(SLOTS, 128) for h in range(2)], axis=1)[:, :width]
    picked = lax.dot_general(
        returned, sel[...], (((0,), (0,)), ((), ())), preferred_element_type=jnp.float32
    )
    out_ref[...] = (picked * score_ref[...]).astype(jnp.bfloat16)

    for copy in started:
        copy.wait_send()
    for sem in (a_send, r_send):

        @pl.when(mixed == 1)
        def _():
            pltpu.make_async_copy(outgoing, outgoing, sem).wait()

        @pl.when(mixed == 0)
        def _():
            most = outgoing.at[:, pl.ds(0, EXPERTS - 1)]
            pltpu.make_async_copy(most, most, sem).wait()


def per_device(tokens, route, gate_score, w_gate, w_up, w_down):
    count, width = tokens.shape
    features, units = w_gate.shape[1:]
    bf16, f32 = jnp.bfloat16, jnp.float32
    dma = pltpu.SemaphoreType.DMA
    result = pl.pallas_call(
        kernel,
        out_shape=jax.ShapeDtypeStruct((width, count), bf16),
        in_specs=[pl.BlockSpec(memory_space=pltpu.VMEM)] * 6,
        out_specs=pl.BlockSpec(memory_space=pltpu.VMEM),
        scratch_shapes=[
            pltpu.VMEM((SLOTS, count), bf16),
            pltpu.VMEM((2, EXPERTS, CAP // 4, 4, 128), bf16),
            pltpu.VMEM((2, 2, EXPERTS // 2, CAP // 4, 4, 128), bf16),
            pltpu.VMEM((NY, 2, 2, HALF, 128), bf16),
            pltpu.VMEM((features, units), bf16),
            pltpu.VMEM((features, units), bf16),
            pltpu.VMEM((features, units), bf16),
            pltpu.VMEM((features, units), bf16),
            pltpu.VMEM((NY, 2 * units, WIDE), bf16),
            pltpu.VMEM((NY, units, WIDE), bf16),
            pltpu.VMEM((2, HALF, 2 * units), f32),
            pltpu.VMEM((NY, 2, HALF, units), bf16),
            pltpu.VMEM((HALF, WIDE), f32),
            pltpu.VMEM((2, 2, EXPERTS // 2, CAP // 4, 4, 128), bf16),
            pltpu.VMEM((2, EXPERTS, CAP // 4, 4, 128), bf16),
            dma, dma, dma, dma,
            dma((2, 2, PIECES)), dma((2, 2, PIECES)),
            dma((NY,)), dma((NY,)),
            dma((2, NY)), dma((2, NY)),
            dma((2, NY // 2, 4)), dma((2, NY // 2, 4)),
            dma((2, NY // 2, 4)), dma((2, NY // 2, 4)),
        ],
        compiler_params=pltpu.CompilerParams(collective_id=0, has_side_effects=True),
        name="experts",
    )(tokens.T, route.T, gate_score.T, w_gate[0], w_up[0], w_down[0])
    return result.T


def solution(mesh):
    split = Mesh(mesh.devices.reshape(2, NZ, 2, NY, 2), EXPERT + BLK)
    return jax.shard_map(
        per_device,
        mesh=split,
        in_specs=(
            P(EXPERT, BLK),
            P(EXPERT, None),
            P(EXPERT, None),
            P(EXPERT, None, BLK),
            P(EXPERT, None, BLK),
            P(EXPERT, BLK, None),
        ),
        out_specs=P(EXPERT, BLK),
        check_vma=False,
    )
```

time: 319 us -> 134 us (0.42)
  waiting for transfers between devices: 178 us -> 0 us
  Pallas kernels: 0 us -> 132 us
  blocking collectives: 104 us -> 0 us
  matrix products: 17.9 us -> 0 us
  between operations: 13.2 us -> 0.01 us
    pallas_call x0 -> x1, Pallas kernels: none -> 132 us  [per_device(): pl.pallas_call(kernel, out_shape=jax.ShapeDtypeStruct((width, count), bf1...]
    reduce_scatter x2 -> x0, waiting for transfers between devices: 108 us -> none  [summed_rows(): nearer = lax.psum_scatter(value, axes[0], scatter_dimension=dim, tiled=True)]
    all_to_all x4 -> x0, blocking collectives: 93.5 us -> none  [exchange_in_order(): result = lax.all_to_all(result, axes[k], k, k, tiled=True)]
    all_gather x1 -> x0, waiting for transfers between devices: 69.6 us -> none  [whole_of(): nearer = lax.all_gather(value, axes[-1], axis=dim, tiled=True)]
    dot_general x4 -> x0, matrix products: 17.9 us -> none  [the longest x1 10.8 us: per_device(): partial_sum = jnp.dot(hidden, down_rows, preferred_element_type=jnp.float32)]
    all_gather x1 -> x0, blocking collectives: 10.6 us -> none  [whole_of(): nearer = lax.all_gather(value, axes[-1], axis=dim, tiled=True)]
  transfers between devices with their start and end apart: 3 -> 0, of which waited for: 3 -> 0; matrix products, arithmetic and copies ran while one was open for 0% -> 0% of each run, Pallas kernels for 0% -> 0%
where the time goes in v1:
time: 134 us; the launch traced here: 133 us
  Pallas kernels  132 us (99%)
  local copies, waits for them, and re-layouts  1.64 us (1%)
    pallas_call x1, Pallas kernels, per_device(): pl.pallas_call(kernel, out_shape=jax.ShapeDtypeStruct((width, count), bf1...  132 us

profile of v1, /device:TPU:1, one launch (start us, length us, event | category | flops | bytes accessed | tf_op | source)
XLA Modules:
  0.0 133.4 jit_solution(16734627586143696866)
XLA Ops:
  0.0 131.7 %experts.1 = bf16[224,512]{1,0:T(8,128)(2,1)} custom-call(bf16[224,512]{1,0:T(8,128)(2,1)} %bitcast.11, s32[1,512]{1,0:T(1,128)} %bitcast.12, f32[1,512]{1,0:T(1,128)} %bitcast.13, bf16[3584,128]{1,0:T(8,128)(2,1)} %bitcast.8, bf16[3584,128]{1,0:T(8,128)(2,1)} %bitcast.9, bf16[128,3584]{1,0:T(8,128)(2,1)} %bitcast.10), custom_call_target="tpu_custom_call" | custom-call | tf_op jit(solution)/shard_map/experts/pallas_call | solution.py:328
  131.8 1.6 %copy.8 = bf16[512,224]{0,1:T(8,128)(2,1)} copy(bf16[512,224]{0,1:T(8,128)(2,1)} %bitcast.7) | data formatting | bytes 458752

commit v2 on v1

v2 whole, which is shorter than its diff:
```python
import functools

import jax
import jax.numpy as jnp
from jax import lax
from jax.experimental import pallas as pl
from jax.experimental.pallas import tpu as pltpu
from jax.sharding import Mesh
from jax.sharding import PartitionSpec as P

EXPERT = ("xl", "z", "core")
BLK = ("y", "xh")
MESH = pl.DeviceIdType.MESH
NZ, NY = 16, 8
EXPERTS, CAP = 64, 12
SLOTS = EXPERTS * CAP
HALF = SLOTS // 2
WIDE = 512
PIECES = 8
EARLY = 3
PACK = 4


def remote(src, dst, send, recv, device):
    return pltpu.make_async_remote_copy(
        src_ref=src, dst_ref=dst, send_sem=send, recv_sem=recv, device_id=device, device_id_type=MESH
    )


def padded_halves(rows, groups):
    width = rows.shape[1]
    low = rows[:, :128]
    high = jnp.concatenate([rows[:, 128:], jnp.zeros((rows.shape[0], 256 - width), rows.dtype)], axis=1)
    return [part.reshape(groups, CAP // 4, 4, 128) for part in (low, high)]


def kernel(
    tok_ref, route_ref, score_ref, wg_ref, wu_ref, wd_ref, out_ref,
    sel, outgoing, arrived, low, high, wg, wu, wg2, wu2, wd2, acc, hidden, total, leaving, back,
    a_send, a_recv, r_send, r_recv, w_load, w_send, w_recv, d_send, d_recv, x_send, x_recv,
    ring_send, ring_recv, hid_send, hid_recv, round_sem,
):
    xl, z, c = lax.axis_index("xl"), lax.axis_index("z"), lax.axis_index("core")
    y, xh = lax.axis_index("y"), lax.axis_index("xh")
    width = tok_ref.shape[0]
    opposite = (xl, z, c, y, 1 - xh)
    up, down = lax.rem(y + 1, NY), lax.rem(y + NY - 1, NY)
    above, below = (xl, z, c, up, xh), (xl, z, c, down, xh)
    mixed = lax.rem(c + xh, 2)
    started = []

    def start(copy):
        copy.start()
        started.append(copy)

    loads = [
        pltpu.make_async_copy(wg_ref, wg, w_load.at[0]),
        pltpu.make_async_copy(wu_ref, wu, w_load.at[1]),
    ]
    for copy in loads:
        copy.start()

    barrier = pltpu.get_barrier_semaphore()
    ahead, behind = (xl, lax.rem(z + 1, NZ), c, y, xh), (xl, lax.rem(z + NZ - 1, NZ), c, y, xh)
    near = [ahead, behind]
    for k in range(1, 8):
        near.append((lax.rem(xl + k // 4, 2), z, lax.rem(c + k // 2 % 2, 2), y, lax.rem(xh + k % 2, 2)))
    for k in range(1, NY):
        near.append((xl, z, c, lax.rem(y + k, NY), xh))
    for device in near:
        pl.semaphore_signal(barrier, inc=1, device_id=device, device_id_type=MESH)

    count = tok_ref.shape[1]
    target = route_ref[...]
    named = lax.broadcasted_iota(jnp.int32, (EXPERTS, count), 0) == target
    earlier = lax.broadcasted_iota(jnp.int32, (count, count), 0) < lax.broadcasted_iota(
        jnp.int32, (count, count), 1
    )
    before = jnp.dot(
        jnp.where(named, 1.0, 0.0).astype(jnp.bfloat16),
        jnp.where(earlier, 1.0, 0.0).astype(jnp.bfloat16),
        preferred_element_type=jnp.float32,
    )
    rank = jnp.sum(jnp.where(named, before, 0.0), axis=0, keepdims=True)
    slot = target.astype(jnp.float32) * CAP + rank
    place = lax.broadcasted_iota(jnp.int32, (SLOTS, count), 0).astype(jnp.float32)
    sel[...] = jnp.where(place == slot, 1.0, 0.0).astype(jnp.bfloat16)
    slotted = lax.dot_general(
        sel[...], tok_ref[...], (((1,), (1,)), ((), ())), preferred_element_type=jnp.float32
    ).astype(jnp.bfloat16)
    for h, part in enumerate(padded_halves(slotted, EXPERTS)):
        outgoing[h] = part

    pl.semaphore_wait(barrier, len(near))

    own_rows = pl.ds(pl.multiple_of(128 * xh, 128), 128)
    other_rows = pl.ds(pl.multiple_of(128 * (1 - xh), 128), 128)

    def columns_of(yy):
        return pl.ds(pl.multiple_of(128 * (7 * (yy // 2) + 3 * lax.rem(yy, 2)), 128), WIDE)

    kept = pltpu.make_async_copy(wd_ref.at[:, columns_of(y)], wd2.at[y, own_rows], d_recv.at[0])
    kept.start()
    for k in (4, 3, 5, 2, 6, 1, 7):
        yy = lax.rem(y + k, NY)
        copy = remote(
            wd_ref.at[:, columns_of(yy)], wd2.at[y, own_rows], d_send.at[k], d_recv.at[k], (xl, z, c, yy, xh)
        )
        start(copy)

    part_rows = wg_ref.shape[0] // PIECES

    def weight_copies(p):
        piece = pl.ds(part_rows * p, part_rows)
        return (
            remote(wg_ref.at[piece], wg2.at[piece], w_send.at[0, p], w_recv.at[0, p], opposite),
            remote(wu_ref.at[piece], wu2.at[piece], w_send.at[1, p], w_recv.at[1, p], opposite),
        )

    for p in range(EARLY):
        start(weight_copies(p)[0])

    mine = xl * NZ + z

    def dispatch(zz, here):
        for a in range(2):
            for b in range(2):
                xx, cc = lax.rem(xl + a, 2), lax.rem(c + b, 2)
                src = outgoing.at[:, (xx * NZ + zz) * 2 + cc]
                dst = arrived.at[xh, :, mine]
                away = remote(src, dst, a_send, a_recv, (xx, zz, cc, y, c))
                if here and a == 0 and b == 0:
                    pl.when(mixed == 1)(away.start)

                    @pl.when(mixed == 0)
                    def _():
                        pltpu.make_async_copy(src, dst, a_recv).start()
                else:
                    away.start()

    dispatch(z, True)

    def next_round(r, carry):
        for device in (ahead, behind):
            pl.semaphore_signal(round_sem.at[r], inc=1, device_id=device, device_id_type=MESH)
        pl.semaphore_wait(round_sem.at[r], 2)
        dispatch(lax.rem(z + r + 1, NZ), False)
        dispatch(lax.rem(z + NZ - 1 - r, NZ), False)
        return carry

    lax.fori_loop(0, NZ // 2 - 1, next_round, 0)
    last = NZ // 2 - 1
    for device in (ahead, behind):
        pl.semaphore_signal(round_sem.at[last], inc=1, device_id=device, device_id_type=MESH)
    pl.semaphore_wait(round_sem.at[last], 2)
    dispatch(lax.rem(z + NZ // 2, NZ), False)

    for p in range(PIECES):
        for which, copy in enumerate(weight_copies(p)):
            if which == 1 or p >= EARLY:
                start(copy)

    def far_first(k):
        return lax.rem(z + NZ // 2 + (1 - 2 * lax.rem(k, 2)) * ((k + 1) // 2) + NZ, NZ)

    pltpu.make_async_copy(arrived, arrived, a_recv).wait()
    block = HALF // PACK
    rest = width - 128
    for s in range(2):
        low[y, s] = arrived[s, 0].reshape(HALF, 128)
        upper = arrived[s, 1].reshape(HALF, 128)
        high[y, s] = jnp.concatenate(
            [upper[block * i : block * (i + 1), :rest] for i in range(PACK)], axis=1
        )

    def ring(view, subs, send, recv, work):
        def hop(origin, s, d, j):
            there = above if d == 0 else below
            return remote(view(origin, j), view(origin, j), send.at[d, s, j], recv.at[d, s, j], there)

        for j in range(subs):
            for d in range(2):
                start(hop(y, 0, d, j))
        work(0, y, None)
        for s in range(1, NY // 2 + 1):
            origins = (lax.rem(y - s + NY, NY), lax.rem(y + s, NY))
            for j in range(subs):
                for d in range(2):
                    whole_way = (j < subs // 2) == (d == 0)
                    if s == NY // 2 and not whole_way:
                        continue
                    hop(origins[d], s - 1, d, j).wait_recv()
                    if s < NY // 2 - 1 or (s == NY // 2 - 1 and whole_way):
                        start(hop(origins[d], s, d, j))
            if s < NY // 2:
                work(s, *origins)
            else:
                work(s, origins[0], None)

    def gate_up(origin, which, g_ref, u_ref):
        result = acc[which]
        for s in range(2):
            first_row = pl.ds(pl.multiple_of((2 * origin + s) * width, 32), width)
            packed = high[origin, s]
            upper = jnp.concatenate([packed[:, rest * i : rest * (i + 1)] for i in range(PACK)], axis=0)
            values = jnp.concatenate([low[origin, s], upper], axis=1)
            weights = jnp.concatenate([g_ref[first_row, :], u_ref[first_row, :]], axis=1)
            result = result + jnp.dot(values, weights, preferred_element_type=jnp.float32)
        acc[which] = result

    def first_work(s, one, two):
        if s == 0:
            acc[...] = jnp.zeros_like(acc)
            for copy in loads:
                copy.wait()
        fresh = (one,) if two is None else (one, two)
        for origin in fresh:
            gate_up(origin, 0, wg, wu)
        if s == 1:
            for k in range(NY):
                wait_spread(k)
            for p in range(NY):
                start(across(p))
        if s == NY // 2 - 1:
            for p in range(PIECES):
                for copy in weight_copies(p):
                    copy.wait_recv()
            lax.fori_loop(NY // 2 + 2, NY + NY // 2 - 1, other_units, 0)
        if s == NY // 2:
            lax.fori_loop(NY // 2 - 1, NY // 2 + 2, other_units, 0)

    def other_units(k, carry):
        gate_up(lax.rem(y + k, NY), 1, wg2, wu2)
        return carry

    def wait_spread(k):
        source = lax.rem(y - k + NY, NY)
        dst = wd2.at[source, own_rows]
        pltpu.make_async_copy(dst, dst, d_recv.at[k]).wait()

    def across(p):
        return remote(wd2.at[p, own_rows], wd2.at[p, own_rows], x_send.at[p], x_recv.at[p], opposite)

    ring(
        lambda origin, j: (low, high)[j % 2].at[origin, j // 2], 4, ring_send, ring_recv, first_work
    )

    for which, plane in ((0, xh), (1, 1 - xh)):
        gate, value = acc[which, :, :128], acc[which, :, 128:]
        hidden[y, plane] = (gate / (1.0 + jnp.exp(-gate)) * value).astype(jnp.bfloat16)

    def project(origin):
        values = jnp.concatenate([hidden[origin, 0], hidden[origin, 1]], axis=1)
        total[...] += jnp.dot(values, wd2[origin], preferred_element_type=jnp.float32)

    def projections(k, carry):
        project(lax.rem(y + k, NY))
        return carry

    def second_work(s, one, two):
        if s == 0:
            total[...] = jnp.zeros_like(total)
        if s == NY // 2 - 1:
            for p in range(NY):
                dst = wd2.at[p, other_rows]
                pltpu.make_async_copy(dst, dst, x_recv.at[p]).wait()
            lax.fori_loop(NY // 2 + 2, NY + NY // 2 - 1, projections, 0)
        if s == NY // 2:
            lax.fori_loop(NY // 2 - 1, NY // 2 + 2, projections, 0)

    ring(
        lambda origin, j: hidden.at[origin, j // 2, pl.ds(HALF // 2 * (j % 2), HALF // 2)],
        4, hid_send, hid_recv, second_work,
    )
    summed = total[...]
    summed = jnp.where(lax.rem(y, 2) == 1, summed[:, WIDE - 2 * width :], summed[:, : 2 * width])
    for s in range(2):
        share = summed[:, s * width : (s + 1) * width].astype(jnp.bfloat16)
        for h, part in enumerate(padded_halves(share, EXPERTS // 2)):
            leaving[s, h] = part

    expert = mine * 2 + c

    def give_back(k, carry):
        zz = far_first(k)
        for a in range(2):
            for b in range(2):
                xx, there = lax.rem(xl + a, 2), lax.rem(xh + b, 2)
                src = leaving.at[there, :, xx * NZ + zz]
                dst = back.at[:, expert]
                away = remote(src, dst, r_send, r_recv, (xx, zz, xh, y, there))
                if a == 0 and b == 0:
                    pl.when((NZ - 1 - k) + mixed > 0)(away.start)

                    @pl.when((NZ - 1 - k) + mixed == 0)
                    def _():
                        pltpu.make_async_copy(src, dst, r_recv).start()
                else:
                    away.start()
        return carry

    lax.fori_loop(0, NZ, give_back, 0)
    pltpu.make_async_copy(back, back, r_recv).wait()
    returned = jnp.concatenate([back[h].reshape(SLOTS, 128) for h in range(2)], axis=1)[:, :width]
    picked = lax.dot_general(
        returned, sel[...], (((0,), (0,)), ((), ())), preferred_element_type=jnp.float32
    )
    out_ref[...] = (picked * score_ref[...]).astype(jnp.bfloat16)

    for copy in started:
        copy.wait_send()
    for sem in (a_send, r_send):

        @pl.when(mixed == 1)
        def _():
            pltpu.make_async_copy(outgoing, outgoing, sem).wait()

        @pl.when(mixed == 0)
        def _():
            most = outgoing.at[:, pl.ds(0, EXPERTS - 1)]
            pltpu.make_async_copy(most, most, sem).wait()


def per_device(tokens, route, gate_score, w_gate, w_up, w_down):
    count, width = tokens.shape
    features, units = w_gate.shape[1:]
    bf16, f32 = jnp.bfloat16, jnp.float32
    dma = pltpu.SemaphoreType.DMA
    result = pl.pallas_call(
        kernel,
        out_shape=jax.ShapeDtypeStruct((width, count), bf16),
        in_specs=[pl.BlockSpec(memory_space=pltpu.VMEM)] * 3 + [pl.BlockSpec(memory_space=pl.ANY)] * 3,
        out_specs=pl.BlockSpec(memory_space=pltpu.VMEM),
        scratch_shapes=[
            pltpu.VMEM((SLOTS, count), bf16),
            pltpu.VMEM((2, EXPERTS, CAP // 4, 4, 128), bf16),
            pltpu.VMEM((2, 2, EXPERTS // 2, CAP // 4, 4, 128), bf16),
            pltpu.VMEM((NY, 2, HALF, 128), bf16),
            pltpu.VMEM((NY, 2, HALF // PACK, PACK * (width - 128)), bf16),
            pltpu.VMEM((features, units), bf16),
            pltpu.VMEM((features, units), bf16),
            pltpu.VMEM((features, units), bf16),
            pltpu.VMEM((features, units), bf16),
            pltpu.VMEM((NY, 2 * units, WIDE), bf16),
            pltpu.VMEM((2, HALF, 2 * units), f32),
            pltpu.VMEM((NY, 2, HALF, units), bf16),
            pltpu.VMEM((HALF, WIDE), f32),
            pltpu.VMEM((2, 2, EXPERTS // 2, CAP // 4, 4, 128), bf16),
            pltpu.VMEM((2, EXPERTS, CAP // 4, 4, 128), bf16),
            dma, dma, dma, dma,
            dma((2,)), dma((2, PIECES)), dma((2, PIECES)),
            dma((NY,)), dma((NY,)),
            dma((NY,)), dma((NY,)),
            dma((2, NY // 2, 4)), dma((2, NY // 2, 4)),
            dma((2, NY // 2, 4)), dma((2, NY // 2, 4)),
            pltpu.SemaphoreType.REGULAR((NZ // 2,)),
        ],
        compiler_params=pltpu.CompilerParams(collective_id=0, has_side_effects=True),
        name="experts",
    )(tokens.T, route.T, gate_score.T, w_gate[0], w_up[0], w_down[0])
    return result.T


def solution(mesh):
    split = Mesh(mesh.devices.reshape(2, NZ, 2, NY, 2), EXPERT + BLK)
    return jax.shard_map(
        per_device,
        mesh=split,
        in_specs=(
            P(EXPERT, BLK),
            P(EXPERT, None),
            P(EXPERT, None),
            P(EXPERT, None, BLK),
            P(EXPERT, None, BLK),
            P(EXPERT, BLK, None),
        ),
        out_specs=P(EXPERT, BLK),
        check_vma=False,
    )
```

time: 134 us -> 118 us (0.88)
  Pallas kernels: 132 us -> 116 us
    pallas_call x1, Pallas kernels: 132 us -> 116 us  [per_device(): pl.pallas_call(kernel, out_shape=jax.ShapeDtypeStruct((width, count), bf1...]
where the time goes in v2:
time: 118 us
  Pallas kernels  116 us (98%)
  local copies, waits for them, and re-layouts  1.64 us (1%)
    pallas_call x1, Pallas kernels, per_device(): pl.pallas_call(kernel, out_shape=jax.ShapeDtypeStruct((width, count), bf1...  116 us

profile of v2, /device:TPU:1, one launch (start us, length us, event | category | flops | bytes accessed | tf_op | source)
XLA Modules:
  0.0 118.1 jit_solution(2995154885967558324)
XLA Ops:
  0.0 116.5 %experts.1 = bf16[224,512]{1,0:T(8,128)(2,1)} custom-call(bf16[224,512]{1,0:T(8,128)(2,1)} %bitcast.11, s32[1,512]{1,0:T(1,128)} %bitcast.12, f32[1,512]{1,0:T(1,128)} %bitcast.13, bf16[3584,128]{1,0:T(8,128)(2,1)} %bitcast.8, bf16[3584,128]{1,0:T(8,128)(2,1)} %bitcast.9, bf16[128,3584]{1,0:T(8,128)(2,1)} %bitcast.10), custom_call_target="tpu_custom_call" | custom-call | tf_op jit(solution)/shard_map/experts/pallas_call | solution.py:329
  116.5 1.6 %copy.8 = bf16[512,224]{0,1:T(8,128)(2,1)} copy(bf16[512,224]{0,1:T(8,128)(2,1)} %bitcast.7) | data formatting | bytes 458752

commit v3 on v2

--- a/solution.py
+++ b/solution.py
@@ -166,19 +166,24 @@
     pltpu.make_async_copy(arrived, arrived, a_recv).wait()
     block = HALF // PACK
     rest = width - 128
-    for s in range(2):
-        low[y, s] = arrived[s, 0].reshape(HALF, 128)
-        upper = arrived[s, 1].reshape(HALF, 128)
-        high[y, s] = jnp.concatenate(
-            [upper[block * i : block * (i + 1), :rest] for i in range(PACK)], axis=1
-        )
-
-    def ring(view, subs, send, recv, work):
+
+    def plain_rows(j):
+        half = arrived[j // 2, j % 2].reshape(HALF, 128)
+        if j % 2 == 0:
+            low[y, j // 2] = half
+        else:
+            high[y, j // 2] = jnp.concatenate(
+                [half[block * i : block * (i + 1), :rest] for i in range(PACK)], axis=1
+            )
+
+    def ring(view, subs, send, recv, work, prepare=None):
         def hop(origin, s, d, j):
             there = above if d == 0 else below
             return remote(view(origin, j), view(origin, j), send.at[d, s, j], recv.at[d, s, j], there)
 
         for j in range(subs):
+            if prepare is not None:
+                prepare(j)
             for d in range(2):
                 start(hop(y, 0, d, j))
         work(0, y, None)
@@ -242,7 +247,8 @@
         return remote(wd2.at[p, own_rows], wd2.at[p, own_rows], x_send.at[p], x_recv.at[p], opposite)
 
     ring(
-        lambda origin, j: (low, high)[j % 2].at[origin, j // 2], 4, ring_send, ring_recv, first_work
+        lambda origin, j: (low, high)[j % 2].at[origin, j // 2], 4, ring_send, ring_recv, first_work,
+        plain_rows,
     )
 
     for which, plane in ((0, xh), (1, 1 - xh)):

time: 118 us -> 118 us (level)
  no operation moved by 1% of the time
where the time goes in v3:
time: 118 us
  Pallas kernels  116 us (98%)
  local copies, waits for them, and re-layouts  1.64 us (1%)
    pallas_call x1, Pallas kernels, per_device(): pl.pallas_call(kernel, out_shape=jax.ShapeDtypeStruct((width, count), bf1...  116 us

profile of v3, /device:TPU:1, one launch (start us, length us, event | category | flops | bytes accessed | tf_op | source)
XLA Modules:
  0.0 118.1 jit_solution(13226845372960151360)
XLA Ops:
  0.0 116.5 %experts.1 = bf16[224,512]{1,0:T(8,128)(2,1)} custom-call(bf16[224,512]{1,0:T(8,128)(2,1)} %bitcast.11, s32[1,512]{1,0:T(1,128)} %bitcast.12, f32[1,512]{1,0:T(1,128)} %bitcast.13, bf16[3584,128]{1,0:T(8,128)(2,1)} %bitcast.8, bf16[3584,128]{1,0:T(8,128)(2,1)} %bitcast.9, bf16[128,3584]{1,0:T(8,128)(2,1)} %bitcast.10), custom_call_target="tpu_custom_call" | custom-call | tf_op jit(solution)/shard_map/experts/pallas_call | solution.py:335
  116.5 1.6 %copy.8 = bf16[512,224]{0,1:T(8,128)(2,1)} copy(bf16[512,224]{0,1:T(8,128)(2,1)} %bitcast.7) | data formatting | bytes 458752
